TPU v7x, 512 devices: a whole 4x4x16 slice. The times are simulated.
512 devices in a mesh: layer: 32 (over x, z_lo, core), row: 4 (over y), col: 4 (over z_hi).
Axes of the slice: x: 4, y: 4, z: 16 (z_hi: 4, z_lo: 4; z = z_hi * 4 + z_lo), core: 2. Of those that a mesh axis runs over, the one named last changes fastest.
Arguments:
- reflect_fwd: float32 [32, 1024, 1024], P('layer', 'row', 'col'), may hold values from -1 to 1
- transmit_fwd: float32 [32, 1024, 1024], P('layer', 'row', 'col'), may hold values from -1 to 1
- reflect_bwd: float32 [32, 1024, 1024], P('layer', 'row', 'col'), may hold values from -1 to 1
- transmit_bwd: float32 [32, 1024, 1024], P('layer', 'row', 'col'), may hold values from -1 to 1
- material_ids: int32 [32], P('layer'), may hold values from 0 to 7
- interface_gain: float32 [8, 1024], replicated, may hold values from 0.5 to 1
Outputs:
- reflect_out: float32 [32, 1024, 1024], P('layer', 'row', 'col')
- transmit_out: float32 [32, 1024, 1024], P('layer', 'row', 'col')
All inputs are finite; a program needn't handle non-finite values.
Results may differ from a plain program's by a relative error of at most 0.00015.
Values sent between devices are 32-bit elements; how exact they have to be, the bound alone decides.
A program may use at most 64 MiB of HBM per device.

v0:
```python
import jax
import jax.numpy as jnp
from jax import lax
from jax.sharding import PartitionSpec as P

NTERMS = 6


PRECISE = lax.Precision.HIGHEST


def partner(block, axis, stride):
    count = lax.axis_size(axis)
    route = []
    for low in range(count):
        high = low | 1 << stride
        if high != low and high < count:
            route += [(low, high), (high, low)]
    return lax.ppermute(block, axis, route)


def folder(panel, incoming):
    return jnp.dot(panel, incoming, precision=PRECISE, preferred_element_type=jnp.float32)


def folder_pair(first_panel, second_panel, incoming):
    return (
        jnp.dot(first_panel, incoming, precision=PRECISE, preferred_element_type=jnp.float32),
        jnp.dot(second_panel, incoming, precision=PRECISE, preferred_element_type=jnp.float32),
    )


def on_device(reflect_fwd, transmit_fwd, reflect_bwd, transmit_bwd, material_ids, interface_gain):
    reflect_own = reflect_fwd[0]
    transmit_own = transmit_fwd[0]
    reflect_back = reflect_bwd[0]
    transmit_back = transmit_bwd[0]
    rows_blk = reflect_own.shape[0]
    cols_blk = reflect_own.shape[1]
    materials = interface_gain.shape[0]
    selector = (material_ids[0] == jnp.arange(materials, dtype=jnp.int32)).astype(jnp.float32)
    own_gain = jnp.dot(selector[None, :], interface_gain, precision=PRECISE)[0]
    distance = lax.axis_size("layer") // 2
    partner_bit = distance.bit_length() - 1
    upper_side = lax.axis_index("layer") < distance
    other_reflect, other_transmit, other_back, other_tback, partner_gain = partner(
        (reflect_own, transmit_own, reflect_back, transmit_back, own_gain), "layer", partner_bit
    )
    reflect_a = jnp.where(upper_side, reflect_own, other_reflect)
    transmit_a = jnp.where(upper_side, transmit_own, other_transmit)
    back_a = jnp.where(upper_side, reflect_back, other_back)
    tback_a = jnp.where(upper_side, transmit_back, other_tback)
    reflect_b = jnp.where(upper_side, other_reflect, reflect_own)
    transmit_b = jnp.where(upper_side, other_transmit, transmit_own)
    weight = own_gain * partner_gain
    row_index = lax.axis_index("row")
    col_index = lax.axis_index("col")
    row_gain = lax.dynamic_slice_in_dim(weight, row_index * rows_blk, rows_blk)
    col_gain = lax.dynamic_slice_in_dim(weight, col_index * cols_blk, cols_blk)
    scaled_fwd = row_gain[:, None] * transmit_a
    scaled_bwd = tback_a * col_gain[None, :]
    global_rows = lax.broadcasted_iota(jnp.int32, (rows_blk, cols_blk), 0) + row_index * rows_blk
    global_cols = lax.broadcasted_iota(jnp.int32, (rows_blk, cols_blk), 1) + col_index * cols_blk
    eye_block = (global_rows == global_cols).astype(jnp.float32)
    back_rows, bwd_rows = (
        lax.all_gather(back_a, "col", axis=1, tiled=True),
        lax.all_gather(scaled_bwd, "col", axis=1, tiled=True),
    )
    power_term, side_term = folder_pair(
        back_rows, bwd_rows, lax.all_gather(reflect_b, "row", axis=0, tiled=True)
    )
    power_rows = lax.all_gather(power_term, "col", axis=1, tiled=True)
    series = eye_block + power_term
    for repeat in range(NTERMS - 2):
        series = eye_block + folder(power_rows, lax.all_gather(series, "row", axis=0, tiled=True))
    series_panel = lax.all_gather(series, "col", axis=1, tiled=True)
    middle = folder(series_panel, lax.all_gather(scaled_fwd, "row", axis=0, tiled=True))
    lower_rows, side_rows = (
        lax.all_gather(transmit_b, "col", axis=1, tiled=True),
        lax.all_gather(side_term, "col", axis=1, tiled=True),
    )
    trans_out, bounce = folder_pair(
        lower_rows, side_rows, lax.all_gather(middle, "row", axis=0, tiled=True)
    )
    refl_out = reflect_a + bounce
    return (refl_out[None], trans_out[None])


def solution(mesh):
    placed = (
        P("layer", "row", "col"),
        P("layer", "row", "col"),
        P("layer", "row", "col"),
        P("layer", "row", "col"),
        P("layer"),
        P(),
    )
    return jax.shard_map(
        on_device,
        mesh=mesh,
        in_specs=placed,
        out_specs=(P("layer", "row", "col"), P("layer", "row", "col")),
        check_vma=False,
    )
```

profile of v0, /device:TPU:1, one launch (start us, length us, event | category | flops | bytes accessed | tf_op | source)
XLA Modules:
  0.0 630.9 jit_solution(2398933802082771795)
XLA Ops:
  7.2 5.5 collective-permute-start
  12.7 3.9 collective-permute-done
  19.3 4.9 collective-permute-start.3
  24.2 3.7 collective-permute-done.3
  28.7 27.0 %all-gather.16.cloned.1.call-done = f32[1024,256]{1,0:T(8,128)} async-done(((f32[256,256]{1,0:T(8,128)}), f32[1024,256]{1,0:T(8,128)}) %all-gather.16.cloned.1.call-update) | async-done | bytes 1048592 | tf_op jit(solution)/shard_map/all_gather | solution.py:70
  55.8 66.0 %all-gather.20.cloned.1.call-done = f32[256,1024]{1,0:T(8,128)} async-done(((f32[256,256]{1,0:T(8,128)}), f32[256,1024]{1,0:T(8,128)}) %all-gather.20.cloned.1.call-update) | async-done | bytes 1048592 | tf_op jit(solution)/shard_map/all_gather | solution.py:66
  121.8 3.4 convert_add_fusion
  125.8 54.8 %all-gather.22.cloned.1.call-done = f32[256,1024]{1,0:T(8,128)} async-done(((f32[256,256]{1,0:T(8,128)}), f32[256,1024]{1,0:T(8,128)}) %all-gather.22.cloned.1.call-update) | async-done | bytes 1048592 | tf_op jit(solution)/shard_map/all_gather | solution.py:72
  180.6 26.7 %all-gather.24.cloned.1.call-done = f32[1024,256]{1,0:T(8,128)} async-done(((f32[256,256]{1,0:T(8,128)}), f32[1024,256]{1,0:T(8,128)}) %all-gather.24.cloned.1.call-update) | async-done | bytes 1048592 | tf_op jit(solution)/shard_map/all_gather | solution.py:75
  207.3 3.3 convolution_add_fusion.3
  210.7 32.3 %all-gather.26.cloned.1.call-done = f32[1024,256]{1,0:T(8,128)} async-done(((f32[256,256]{1,0:T(8,128)}), f32[1024,256]{1,0:T(8,128)}) %all-gather.26.cloned.1.call-update) | async-done | bytes 1048592 | tf_op jit(solution)/shard_map/all_gather | solution.py:75
  246.0 32.3 %all-gather.28.cloned.1.call-done = f32[1024,256]{1,0:T(8,128)} async-done(((f32[256,256]{1,0:T(8,128)}), f32[1024,256]{1,0:T(8,128)}) %all-gather.28.cloned.1.call-update) | async-done | bytes 1048592 | tf_op jit(solution)/shard_map/all_gather | solution.py:75
  282.2 4.6 collective-permute-start.4
  289.8 4.0 collective-permute-done.2
  294.8 18.8 %all-gather.30.cloned.1.call-done = f32[1024,256]{1,0:T(8,128)} async-done(((f32[256,256]{1,0:T(8,128)}), f32[1024,256]{1,0:T(8,128)}) %all-gather.30.cloned.1.call-update) | async-done | bytes 1048592 | tf_op jit(solution)/shard_map/all_gather | solution.py:75
  317.5 4.6 collective-permute-start.1
  322.1 4.0 collective-permute-done.1
  327.7 20.3 %all-gather.34.cloned.1.call-done = f32[1024,256]{1,0:T(8,128)} async-done(((f32[256,256]{1,0:T(8,128)}), f32[1024,256]{1,0:T(8,128)}) %all-gather.34.cloned.1.call-update) | async-done | bytes 1048592 | tf_op jit(solution)/shard_map/all_gather | solution.py:77
  348.0 66.0 %all-gather.32.cloned.1.call-done = f32[256,1024]{1,0:T(8,128)} async-done(((f32[256,256]{1,0:T(8,128)}), f32[256,1024]{1,0:T(8,128)}) %all-gather.32.cloned.1.call-update) | async-done | bytes 1048592 | tf_op jit(solution)/shard_map/all_gather | solution.py:76
  417.3 54.5 %all-gather.14.cloned.1.call-done = f32[256,1024]{1,0:T(8,128)} async-done(((f32[256,256]{1,0:T(8,128)}), f32[256,1024]{1,0:T(8,128)}) %all-gather.14.cloned.1.call-update) | async-done | bytes 1048592 | tf_op jit(solution)/shard_map/all_gather | solution.py:67
  474.8 54.4 %all-gather.38.cloned.1.call-done = f32[256,1024]{1,0:T(8,128)} async-done(((f32[256,256]{1,0:T(8,128)}), f32[256,1024]{1,0:T(8,128)}) %all-gather.38.cloned.1.call-update) | async-done | bytes 1048592 | tf_op jit(solution)/shard_map/all_gather | solution.py:79
  529.2 26.1 %all-gather.36.cloned.1.call-done = f32[1024,256]{1,0:T(8,128)} async-done(((f32[256,256]{1,0:T(8,128)}), f32[1024,256]{1,0:T(8,128)}) %all-gather.36.cloned.1.call-update) | async-done | bytes 1048592 | tf_op jit(solution)/shard_map/all_gather | solution.py:83
  555.4 3.4 convolution_bitcast_fusion
  558.8 62.7 %all-gather.18.cloned.1.call-done = f32[256,1024]{1,0:T(8,128)} async-done(((f32[256,256]{1,0:T(8,128)}), f32[256,1024]{1,0:T(8,128)}) %all-gather.18.cloned.1.call-update) | async-done | bytes 1048592 | tf_op jit(solution)/shard_map/all_gather | solution.py:80
  (58 shorter events, 29.0 us)
Async XLA Ops:
  7.2 280.3 %copy-start = (f32[8,1024]{1,0:T(8,128)S(1)}, f32[8,1024]{1,0:T(8,128)}, u32[]{:S(2)}) copy-start(f32[8,1024]{1,0:T(8,128)} %param.11) | copy-start | bytes 98308
  7.2 48.6 %all-gather.16.cloned.1.call-start = ((), (), s32[]{:S(2)}) async-start(), calls=%async_computation.1 | async-start | bytes 1310720 | tf_op jit(solution)/shard_map/all_gather | solution.py:70
  7.2 9.4 %collective-permute-start = (f32[256,256]{1,0:T(8,128)}, f32[256,256]{1,0:T(8,128)S(1)}, u32[]{:S(2)}, u32[]{:S(2)}) collective-permute-start(f32[256,256]{1,0:T(8,128)} %bitcast.39), channel_id=1, source_target_pairs={{0,256},{256,0},{16,272},{272,16},{32,288},{288,32},{48,304},{304,... | collective-permute-start | bytes 786440 | tf_op jit(solution)/shard_map/ppermute | solution.py:19
  18.3 0.9 copy-start.7
  18.4 103.4 %all-gather.20.cloned.1.call-start = ((), (), s32[]{:S(2)}) async-start(), calls=%async_computation.3 | async-start | bytes 1310720 | tf_op jit(solution)/shard_map/all_gather | solution.py:66
  19.3 8.6 %collective-permute-start.3 = (f32[256,256]{1,0:T(8,128)S(1)}, f32[256,256]{1,0:T(8,128)S(1)}, u32[]{:S(2)}, u32[]{:S(2)}) collective-permute-start(f32[256,256]{1,0:T(8,128)S(1)} %bitcast.42), channel_id=1, source_target_pairs={{0,256},{256,0},{16,272},{272,16},{32,288},{288,32},{48,304},{304,... | collective-permute-start | bytes 786440 | tf_op jit(solution)/shard_map/ppermute | solution.py:19
  28.7 151.9 %all-gather.22.cloned.1.call-start = ((), (), s32[]{:S(2)}) async-start(), calls=%async_computation.4 | async-start | bytes 1310720 | tf_op jit(solution)/shard_map/all_gather | solution.py:72
  125.2 82.2 %all-gather.24.cloned.1.call-start = ((), (), s32[]{:S(2)}) async-start(), calls=%async_computation.5 | async-start | bytes 1310720 | tf_op jit(solution)/shard_map/all_gather | solution.py:75
  125.7 117.2 %all-gather.26.cloned.1.call-start = ((), (), s32[]{:S(2)}) async-start(), calls=%async_computation.6 | async-start | bytes 1310720 | tf_op jit(solution)/shard_map/all_gather | solution.py:75
  180.6 62.4 %copy-start.1 = (f32[256,1024]{1,0:T(8,128)S(1)}, f32[256,1024]{1,0:T(8,128)}, u32[]{:S(2)}) copy-start(f32[256,1024]{1,0:T(8,128)} %all-gather.22.cloned.1.call-done) | copy-start | bytes 3145732
  210.6 67.7 %all-gather.28.cloned.1.call-start = ((), (), s32[]{:S(2)}) async-start(), calls=%async_computation.7 | async-start | bytes 1310720 | tf_op jit(solution)/shard_map/all_gather | solution.py:75
  245.9 67.7 %all-gather.30.cloned.1.call-start = ((), (), s32[]{:S(2)}) async-start(), calls=%async_computation.8 | async-start | bytes 1310720 | tf_op jit(solution)/shard_map/all_gather | solution.py:75
  281.3 66.7 %all-gather.34.cloned.1.call-start = ((), (), s32[]{:S(2)}) async-start(), calls=%async_computation.10 | async-start | bytes 1310720 | tf_op jit(solution)/shard_map/all_gather | solution.py:77
  282.2 11.7 %collective-permute-start.4 = (f32[256,256]{1,0:T(8,128)S(1)}, f32[256,256]{1,0:T(8,128)S(1)}, u32[]{:S(2)}, u32[]{:S(2)}) collective-permute-start(f32[256,256]{1,0:T(8,128)S(1)} %bitcast.40), channel_id=1, source_target_pairs={{0,256},{256,0},{16,272},{272,16},{32,288},{288,32},{48,304},{304,... | collective-permute-start | bytes 786440 | tf_op jit(solution)/shard_map/ppermute | solution.py:19
  287.6 6.2 collective-permute-start.2
  294.8 119.2 %all-gather.32.cloned.1.call-start = ((), (), s32[]{:S(2)}) async-start(), calls=%async_computation.9 | async-start | bytes 1310720 | tf_op jit(solution)/shard_map/all_gather | solution.py:76
  316.6 155.2 %all-gather.14.cloned.1.call-start = ((), (), s32[]{:S(2)}) async-start(), calls=%async_computation | async-start | bytes 1310720 | tf_op jit(solution)/shard_map/all_gather | solution.py:67
  317.5 8.6 %collective-permute-start.1 = (f32[256,256]{1,0:T(8,128)S(1)}, f32[256,256]{1,0:T(8,128)S(1)}, u32[]{:S(2)}, u32[]{:S(2)}) collective-permute-start(f32[256,256]{1,0:T(8,128)S(1)} %bitcast.41), channel_id=1, source_target_pairs={{0,256},{256,0},{16,272},{272,16},{32,288},{288,32},{48,304},{304,... | collective-permute-start | bytes 786440 | tf_op jit(solution)/shard_map/ppermute | solution.py:19
  326.9 202.3 %all-gather.38.cloned.1.call-start = ((), (), s32[]{:S(2)}) async-start(), calls=%async_computation.12 | async-start | bytes 1310720 | tf_op jit(solution)/shard_map/all_gather | solution.py:79
  327.6 144.2 %copy-start.3 = (f32[1024,256]{1,0:T(8,128)S(1)}, f32[1024,256]{1,0:T(8,128)}, u32[]{:S(2)}) copy-start(f32[1024,256]{1,0:T(8,128)} %all-gather.16.cloned.1.call-done) | copy-start | bytes 3145732
  327.7 227.7 %all-gather.36.cloned.1.call-start = ((), (), s32[]{:S(2)}) async-start(), calls=%async_computation.11 | async-start | bytes 1310720 | tf_op jit(solution)/shard_map/all_gather | solution.py:83
  417.3 204.1 %all-gather.18.cloned.1.call-start = ((), (), s32[]{:S(2)}) async-start(), calls=%async_computation.2 | async-start | bytes 1310720 | tf_op jit(solution)/shard_map/all_gather | solution.py:80
  474.8 146.6 %copy-start.4 = (f32[1,256,256]{2,1,0:T(8,128)S(1)}, f32[1,256,256]{2,1,0:T(8,128)}, u32[]{:S(2)}) copy-start(f32[1,256,256]{2,1,0:T(8,128)} %param.6) | copy-start | bytes 786436
  555.4 66.0 %copy-start.2 = (f32[1024,256]{1,0:T(8,128)S(1)}, f32[1024,256]{1,0:T(8,128)}, u32[]{:S(2)}) copy-start(f32[1024,256]{1,0:T(8,128)} %all-gather.36.cloned.1.call-done) | copy-start | bytes 3145732
  (2 other events, 1.9 us)
Sparse Core Ops, SparseCore 0:
  18.5 37.2 all-gather.15
  58.4 63.3 all-gather.19
  125.3 55.2 all-gather.21
  183.1 24.1 all-gather.23
  210.7 32.1 all-gather.25
  246.1 32.1 all-gather.27
  281.4 32.1 all-gather.29
  315.7 32.1 all-gather.33
  350.7 63.3 all-gather.31
  416.5 55.2 all-gather.13
  473.9 55.2 all-gather.37
  531.2 24.1 all-gather.35
  558.1 63.3 all-gather.17
where the time goes:
time: 632 us; the launch traced here: 631 us
  waiting for transfers between devices  559 us (88%)
  matrix products  28.1 us (4%)
  starting transfers between devices  22.2 us (4%)
  between operations  14.7 us (2%)
    all_gather x4, waiting for transfers between devices, on_device(): lax.all_gather(series, 'row', axis=0, tiled=True)  110 us
    all_gather x1, waiting for transfers between devices, on_device(): series_panel = lax.all_gather(series, 'col', axis=1, tiled=True)  66 us
    all_gather x1, waiting for transfers between devices, on_device(): lax.all_gather(back_a, 'col', axis=1, tiled=True)  66 us
    all_gather x1, waiting for transfers between devices, on_device(): lax.all_gather(side_term, 'col', axis=1, tiled=True)  62.7 us
    all_gather x1, waiting for transfers between devices, on_device(): power_rows = lax.all_gather(power_term, 'col', axis=1, tiled=True)  54.8 us
    all_gather x1, waiting for transfers between devices, on_device(): lax.all_gather(scaled_bwd, 'col', axis=1, tiled=True)  54.5 us
    all_gather x1, waiting for transfers between devices, on_device(): lax.all_gather(transmit_b, 'col', axis=1, tiled=True)  54.4 us
    all_gather x1, waiting for transfers between devices, on_device(): lax.all_gather(reflect_b, 'row', axis=0, tiled=True)  27 us
  transfers between devices with their start and end apart: 18, of which 17 were waited for; matrix products, arithmetic and copies ran while one was open for 2% of the time, Pallas kernels for 0%

commit v1 on v0

v1 whole, which is shorter than its diff:
```python
import jax
import jax.numpy as jnp
from jax import lax
from jax.experimental import pallas as pl
from jax.experimental.pallas import tpu as pltpu
from jax.sharding import PartitionSpec as P

NTERMS = 6
MESH = pl.DeviceIdType.MESH
F32 = jnp.float32
BF16 = jnp.bfloat16
ORDER = (0, 3, 1, 2)

Z_RB, Z_TB, Z_RF, Z_TF, Z_FT, Z_WA, Z_WB = 0, 1, 2, 3, 4, 8, 9
R_RB, R_TB, R_TF, R_SS, R_RF, R_MT, R_PA, R_PB = 10, 14, 18, 22, 26, 30, 34, 38
C_RF, C_MT, C_PP = 54, 58, 62
O_PRIM, O_SEC, O_RA = 78, 80, 82
N_RECV = 83
N_SEND = 120

NN = (((1,), (0,)), ((), ()))
NT = (((1,), (1,)), ((), ()))


def split(value):
    high = value.astype(BF16)
    low = (value - high.astype(F32)).astype(BF16)
    return high, low


def dot3(left, right, dims):
    lh, ll = left
    rh, rl = right

    def one(a, b):
        return lax.dot_general(a, b, dims, preferred_element_type=F32)

    return one(lh, rh) + (one(lh, rl) + one(ll, rh))


def kernel(rf_ref, tf_ref, rb_ref, tb_ref, mid_ref, gain_ref,
           prim_ref, sec_ref, ra_ref,
           rb, tb, tf, ss, rf, pp, ph, plo, ft, mt, ot, ob, own_gain, wa, wb, fts,
           ssem, rsem):
    lay = lax.axis_index("layer")
    y = lax.axis_index("row")
    zh = lax.axis_index("col")
    x = lay // 8
    zl = lax.rem(lay // 2, 4)
    c = lax.rem(lay, 2)
    z = zh * 4 + zl
    blk = rf_ref.shape[0]
    half = blk // 2
    quarter = half // 2
    wide = rf.shape[0]
    fine = ft.shape[0]

    upper = x < 2
    zp = lax.rem(zl + 2 + 4 * (2 * lax.rem(x, 2) + c), 16)
    zhp = zp // 4
    zlp = lax.rem(zp, 4)

    def plane(yd, cd):
        return (zh * 8 + zlp * 2 + cd, yd, zhp)

    zz = lax.rem(z + 14, 16)
    sq = zz // 4
    src_lay = (sq // 2) * 8 + lax.rem(zz, 4) * 2 + lax.rem(sq, 2)

    def source(lower, yd):
        return (src_lay + 16 * lower, yd, x)

    def near(xd, yd):
        return (lax.rem(xd, 4) * 8 + zl * 2 + c, lax.rem(yd, 4), zh)

    cross = (lay + 1 - 2 * c, y, zh)
    partner = (lax.rem(lay + 16, 32), y, zh)

    barrier = pltpu.get_barrier_semaphore()

    def signal(device):
        pl.semaphore_signal(barrier, inc=1, device_id=device, device_id_type=MESH)

    for yd in range(4):
        signal(source(0, yd))
    signal(source(1, y))
    for cd in range(2):
        signal(plane(y, cd))
    signal(near(x + 1, y))
    signal(near(x + 3, y))
    signal(near(x, y + 1))
    signal(near(x, y + 3))
    signal(cross)
    signal(partner)

    rows8 = lax.broadcasted_iota(jnp.int32, gain_ref.shape, 0)
    own = jnp.sum(jnp.where(rows8 == mid_ref[0], gain_ref[...], 0.0), axis=0, keepdims=True)
    own_gain[...] = jnp.broadcast_to(own, own_gain.shape)
    fts[...] = tf_ref[...].T

    @pl.when(upper)
    def _():
        pl.semaphore_wait(barrier, 16)

    @pl.when(jnp.logical_not(upper))
    def _():
        pl.semaphore_wait(barrier, 10)

    sends = []
    count = [0]

    def copy_of(src, dst, slot, recv, device):
        return pltpu.make_async_remote_copy(
            src_ref=src, dst_ref=dst, send_sem=ssem.at[slot], recv_sem=rsem.at[recv],
            device_id=device, device_id_type=MESH)

    def send(src, dst, recv, device):
        copy = copy_of(src, dst, count[0], recv, device)
        count[0] += 1
        copy.start()
        sends.append(copy)

    def arrived(dst, recv):
        copy_of(dst, dst, 0, recv, cross).wait_recv()

    def al(index, size):
        return pl.ds(pl.multiple_of(index, size), size)

    mine = al(zh * blk, blk)
    ycols = al(y * blk, blk)

    def upper_moves():
        moves = []
        for cd in range(2):
            moves.append((rb_ref.at[pl.ds(cd * half, half), :], rb.at[:, mine], Z_RB, plane(y, cd)))
        for cd in range(2):
            moves.append((own_gain, wa, Z_WA, plane(y, cd)))
        for yd in range(4):
            for cd in range(2):
                moves.append((fts.at[pl.ds((2 * yd + cd) * fine, fine), :], ft.at[:, ycols], Z_FT + y, plane(yd, cd)))
        for cd in range(2):
            moves.append((tb_ref.at[pl.ds(cd * half, half), :], tb.at[:, mine], Z_TB, plane(y, cd)))
        moves.append((rf_ref, ra_ref, O_RA, partner))
        return moves

    def lower_moves():
        moves = []
        for cd in range(2):
            moves.append((rf_ref.at[pl.ds(cd * half, half), :], rf.at[al((2 * y + cd) * half, half), :], Z_RF, plane(y, cd)))
        for cd in range(2):
            moves.append((own_gain, wb, Z_WB, plane(y, cd)))
        for cd in range(2):
            moves.append((tf_ref.at[pl.ds(cd * half, half), :], tf.at[:, mine], Z_TF, plane(y, cd)))
        return moves

    @pl.when(upper)
    def _():
        for slot, (src, dst, recv, device) in enumerate(upper_moves()):
            copy_of(src, dst, slot, recv, device).start()

    @pl.when(jnp.logical_not(upper))
    def _():
        for slot, (src, dst, recv, device) in enumerate(lower_moves()):
            copy_of(src, dst, slot, recv, device).start()

    count[0] = len(upper_moves())

    class Ring:
        def __init__(self, part, me, device, base):
            self.part, self.me, self.device, self.base = part, me, device, base

        def pos(self, step):
            return lax.rem(self.me + step, 4)

        def start(self):
            piece = self.part(self.me, None)
            send(piece, piece, self.base, self.device(self.me + 1))
            send(piece, piece, self.base + 1, self.device(self.me + 3))

        def left(self):
            arrived(self.part(self.pos(3), None), self.base)
            piece = self.part(self.pos(3), 0)
            send(piece, piece, self.base + 2, self.device(self.me + 1))

        def right(self):
            arrived(self.part(self.pos(1), None), self.base + 1)
            piece = self.part(self.pos(1), 1)
            send(piece, piece, self.base + 3, self.device(self.me + 3))

        def far(self):
            arrived(self.part(self.pos(2), 0), self.base + 2)
            arrived(self.part(self.pos(2), 1), self.base + 3)

    def on_x(a):
        return near(a, y)

    def on_y(a):
        return near(x, a)

    def col_part(buf):
        def part(p, h):
            rows = pl.ds(0, half) if h is None else pl.ds(h * quarter, quarter)
            return buf.at[rows, al(p * blk, blk)]
        return part

    def row_part(buf, size, core):
        def part(p, h):
            start = (2 * p + core) * size
            if h is None:
                return buf.at[al(start, size), :]
            return buf.at[al(start + h * (size // 2), size // 2), :]
        return part

    def cross_send(piece, recv):
        send(piece, piece, recv, cross)

    def cross_wait(part, base):
        for k, step in enumerate(ORDER):
            arrived(part(lax.rem(y + step, 4), None), base + k)

    def y_gather(buf, size, base, cbase):
        part = row_part(buf, size, c)
        ring = Ring(part, y, on_y, base)
        ring.start()
        cross_send(part(y, None), cbase)
        yield
        ring.left()
        cross_send(part(ring.pos(3), None), cbase + 1)
        ring.right()
        cross_send(part(ring.pos(1), None), cbase + 2)
        yield
        ring.far()
        cross_send(part(ring.pos(2), None), cbase + 3)
        cross_wait(row_part(buf, size, 1 - c), cbase)
        yield

    rb_ring = Ring(col_part(rb), x, on_x, R_RB)
    tb_ring = Ring(col_part(tb), x, on_x, R_TB)
    tf_ring = Ring(col_part(tf), x, on_x, R_TF)
    ss_ring = Ring(col_part(ss), x, on_x, R_SS)

    arrived(rb.at[:, al(x * blk, blk)], Z_RB)
    rb_ring.start()
    arrived(rf.at[al((2 * y + c) * half, half), :], Z_RF)
    gather = y_gather(rf, half, R_RF, C_RF)
    next(gather)
    rb_ring.left()
    rb_ring.right()
    next(gather)
    rb_ring.far()
    next(gather)
    right = split(rf[...])
    power = dot3(split(rb[...]), right, NN)

    def mix(a, b, core):
        return a + core * (b - a), b + core * (a - b)

    me_a, me_b = mix(x, y, c)

    def ppart(a, b, h, core):
        jj, ii = mix(a, b, core)
        start = (2 * ii + core) * half
        cols = al(jj * blk, blk)
        if h is None:
            return pp.at[al(start, half), cols]
        return pp.at[al(start + h * quarter, quarter), cols]

    def device_ab(a, b):
        return near(*mix(a, b, c))

    pp[al((2 * y + c) * half, half), al(x * blk, blk)] = power
    ring_a = Ring(lambda p, h: ppart(p, me_b, h, c), me_a, lambda a: device_ab(a, me_b), R_PA)
    rings_b = []
    for k, step in enumerate(ORDER):
        a = lax.rem(me_a + step, 4)
        rings_b.append(Ring(
            lambda p, h, a=a: ppart(a, p, h, c), me_b, lambda b: device_ab(me_a, b), R_PB + 4 * k))

    def start_b(k):
        rings_b[k].start()
        cross_send(rings_b[k].part(me_b, None), C_PP + 4 * k)

    def sides_b(k):
        rings_b[k].left()
        cross_send(rings_b[k].part(rings_b[k].pos(3), None), C_PP + 4 * k + 1)
        rings_b[k].right()
        cross_send(rings_b[k].part(rings_b[k].pos(1), None), C_PP + 4 * k + 2)

    def far_b(k):
        rings_b[k].far()
        cross_send(rings_b[k].part(rings_b[k].pos(2), None), C_PP + 4 * k + 3)

    ring_a.start()
    start_b(0)
    ring_a.left()
    start_b(1)
    ring_a.right()
    start_b(2)
    ring_a.far()
    start_b(3)
    sides_b(0)
    sides_b(1)
    arrived(tb.at[:, al(x * blk, blk)], Z_TB)
    tb_ring.start()
    sides_b(2)
    far_b(0)
    far_b(1)
    sides_b(3)
    arrived(tf.at[:, al(x * blk, blk)], Z_TF)
    tf_ring.start()
    tb_ring.left()
    tb_ring.right()
    far_b(2)
    far_b(3)
    tf_ring.left()
    tf_ring.right()
    tb_ring.far()
    arrived(wa, Z_WA)
    arrived(wb, Z_WB)
    weight = wa[...][0:1, :] * wb[...][0:1, :]
    ss[:, al(x * blk, blk)] = dot3(split(tb[...] * weight), right, NN)
    ss_ring.start()
    oa, obb = mix(x, y, 1 - c)
    for k, step in enumerate(ORDER):
        for m, other in enumerate(ORDER):
            arrived(ppart(lax.rem(oa + step, 4), lax.rem(obb + other, 4), None, 1 - c), C_PP + 4 * k + m)
    for yd in range(4):
        arrived(ft.at[:, pl.ds(yd * blk, blk)], Z_FT + yd)
    ph[...], plo[...] = split(pp[...])
    first = ft[...] * weight

    def horner(step, value):
        return first + dot3(split(value), (ph[...], plo[...]), NT)

    value = lax.fori_loop(0, 2, horner, first)
    ss_ring.left()
    ss_ring.right()
    tf_ring.far()
    value = lax.fori_loop(0, NTERMS - 3, horner, value)
    mt[al((2 * y + c) * fine, fine), :] = value
    gather = y_gather(mt, fine, R_MT, C_MT)
    next(gather)
    ss_ring.far()
    next(gather)
    next(gather)

    middle = split(mt[...])
    ot[...] = dot3(split(tf[...]), middle, NT)
    place = al(c * half, half)
    send(ot, prim_ref.at[place, :], O_PRIM + c, source(1, y))
    ob[...] = dot3(split(ss[...]), middle, NT)
    send(ob, prim_ref.at[place, :], O_PRIM + c, source(0, y))

    for h in range(2):
        piece = prim_ref.at[pl.ds(h * half, half), :]
        arrived(piece, O_PRIM + h)
        send(piece, sec_ref.at[pl.ds(h * half, half), :], O_SEC + h, partner)
    for h in range(2):
        arrived(sec_ref.at[pl.ds(h * half, half), :], O_SEC + h)

    @pl.when(upper)
    def _():
        for slot, (src, dst, recv, device) in enumerate(upper_moves()):
            copy_of(src, dst, slot, recv, device).wait_send()

    @pl.when(jnp.logical_not(upper))
    def _():
        for slot, (src, dst, recv, device) in enumerate(lower_moves()):
            copy_of(src, dst, slot, recv, device).wait_send()
        arrived(ra_ref, O_RA)

    for copy in sends:
        copy.wait_send()
    assert count[0] <= N_SEND


def on_device(reflect_fwd, transmit_fwd, reflect_bwd, transmit_bwd, material_ids, interface_gain):
    blk = reflect_fwd.shape[1]
    order = interface_gain.shape[1]
    half = blk // 2
    fine = order // 32
    anywhere = pl.BlockSpec(memory_space=pl.ANY)
    vmem = pl.BlockSpec(memory_space=pltpu.VMEM)
    shape = jax.ShapeDtypeStruct((blk, blk), F32)
    reflect_own = reflect_fwd[0]
    prim, sec, reflect_peer = pl.pallas_call(
        kernel,
        out_shape=(shape, shape, shape),
        in_specs=[anywhere, vmem, anywhere, anywhere, pl.BlockSpec(memory_space=pltpu.SMEM), vmem],
        out_specs=(anywhere, anywhere, anywhere),
        scratch_shapes=[
            pltpu.VMEM((half, order), F32),
            pltpu.VMEM((half, order), F32),
            pltpu.VMEM((half, order), F32),
            pltpu.VMEM((half, order), F32),
            pltpu.VMEM((order, blk), F32),
            pltpu.VMEM((order, order), F32),
            pltpu.VMEM((order, order), BF16),
            pltpu.VMEM((order, order), BF16),
            pltpu.VMEM((fine, order), F32),
            pltpu.VMEM((blk, order), F32),
            pltpu.VMEM((half, blk), F32),
            pltpu.VMEM((half, blk), F32),
            pltpu.VMEM((8, order), F32),
            pltpu.VMEM((8, order), F32),
            pltpu.VMEM((8, order), F32),
            pltpu.VMEM((blk, blk), F32),
            pltpu.SemaphoreType.DMA((N_SEND,)),
            pltpu.SemaphoreType.DMA((N_RECV,)),
        ],
        compiler_params=pltpu.CompilerParams(
            collective_id=0, has_side_effects=True, vmem_limit_bytes=48 * 1024 * 1024),
        name="star",
    )(reflect_own, transmit_fwd[0], reflect_bwd[0], transmit_bwd[0], material_ids, interface_gain)
    upper = lax.axis_index("layer") < lax.axis_size("layer") // 2
    reflect_a = jnp.where(upper, reflect_own, reflect_peer)
    refl_out = reflect_a + jnp.where(upper, prim, sec)
    trans_out = jnp.where(upper, sec, prim)
    return (refl_out[None], trans_out[None])


def solution(mesh):
    placed = (
        P("layer", "row", "col"),
        P("layer", "row", "col"),
        P("layer", "row", "col"),
        P("layer", "row", "col"),
        P("layer"),
        P(),
    )
    return jax.shard_map(
        on_device,
        mesh=mesh,
        in_specs=placed,
        out_specs=(P("layer", "row", "col"), P("layer", "row", "col")),
        check_vma=False,
    )
```

time: 632 us -> 167 us (0.26)
  the two profiles are of different devices: /device:TPU:1 before, /device:TPU:39 now
where the time goes in v1:
time: 167 us
  Pallas kernels  160 us (96%)
  local copies, waits for them, and re-layouts  4.55 us (3%)
    pallas_call x1, Pallas kernels, on_device(): pl.pallas_call(kernel, out_shape=(shape, shape, shape), in_specs=[anywher...  160 us
    unnamed x10, local copies, waits for them, and re-layouts  4.55 us

profile of v1, /device:TPU:39, one launch (start us, length us, event | category | flops | bytes accessed | tf_op | source)
XLA Modules:
  0.0 166.8 jit_solution(11714420334854966708)
XLA Ops:
  1.3 0.0 copy-start
  1.3 0.9 copy-done
  2.2 0.0 copy-start.1
  2.2 0.9 copy-done.1
  3.2 0.0 copy-start.2
  3.2 0.9 copy-done.2
  4.1 0.0 copy-start.3
  4.1 0.9 copy-done.3
  5.1 0.0 copy-start.4
  5.1 0.8 copy-done.4
  5.8 160.0 %star.1 = (f32[256,256]{1,0:T(8,128)S(1)}, f32[256,256]{1,0:T(8,128)S(1)}, f32[256,256]{1,0:T(8,128)S(1)}) custom-call(f32[256,256]{1,0:T(8,128)S(1)} %bitcast.9, f32[256,256]{1,0:T(8,128)S(1)} %bitcast.10, f32[256,256]{1,0:T(8,128)S(1)} %bitcast.11, f32[256,256]{1,0:T(8,128)S(1)} %bitcast.12, s32[1]{0:T(128)S(6)} %copy.8.mid_ref, f32[8,1024]{1,0:T(8,128)S(1)} %copy-done.4), custom_call_target="tpu_custom_call" | custom-call | tf_op jit(solution)/shard_map/star/pallas_call | solution.py:386
  165.9 0.9 select_bitcast_fusion
Async XLA Ops:
  1.3 1.0 copy-start
  2.2 0.9 copy-start.1
  3.2 0.9 copy-start.2
  4.1 0.9 copy-start.3
  5.1 0.8 copy-start.4

commit v2 on v1

--- a/solution.py
+++ b/solution.py
@@ -11,11 +11,15 @@
 BF16 = jnp.bfloat16
 ORDER = (0, 3, 1, 2)
 
-Z_RB, Z_TB, Z_RF, Z_TF, Z_FT, Z_WA, Z_WB = 0, 1, 2, 3, 4, 8, 9
+PLANE = (13, 10, 2, 4, 8, 1, 14, 6, 11, 3, 7, 12, 5, 15, 9, 0)
+SHIFT = (0, 3, 3, 0, 3, 3, 0, 2, 1, 2, 1, 2, 1, 2, 0, 0)
+
+Z_RB, Z_TB, Z_RF, Z_TF, Z_FT, Z_TR, Z_WA, Z_WB = 0, 1, 2, 3, 4, 5, 8, 9
 R_RB, R_TB, R_TF, R_SS, R_RF, R_MT, R_PA, R_PB = 10, 14, 18, 22, 26, 30, 34, 38
 C_RF, C_MT, C_PP = 54, 58, 62
 O_PRIM, O_SEC, O_RA = 78, 80, 82
-N_RECV = 83
+R_FT = 83
+N_RECV = 87
 N_SEND = 120
 
 NN = (((1,), (0,)), ((), ()))
@@ -38,10 +42,17 @@
     return one(lh, rh) + (one(lh, rl) + one(ll, rh))
 
 
+def lookup(table, index):
+    value = jnp.int32(table[0])
+    for k in range(1, len(table)):
+        value = jnp.where(index == k, jnp.int32(table[k]), value)
+    return value
+
+
 def kernel(rf_ref, tf_ref, rb_ref, tb_ref, mid_ref, gain_ref,
            prim_ref, sec_ref, ra_ref,
            rb, tb, tf, ss, rf, pp, ph, plo, ft, mt, ot, ob, own_gain, wa, wb, fts,
-           ssem, rsem):
+           fv, fr, tr, ssem, rsem, lsem):
     lay = lax.axis_index("layer")
     y = lax.axis_index("row")
     zh = lax.axis_index("col")
@@ -55,23 +66,25 @@
     wide = rf.shape[0]
     fine = ft.shape[0]
 
-    upper = x < 2
-    zp = lax.rem(zl + 2 + 4 * (2 * lax.rem(x, 2) + c), 16)
+    upper = lay < 16
+    pair = lax.rem(lay, 16)
+    zp = lookup(PLANE, pair)
     zhp = zp // 4
     zlp = lax.rem(zp, 4)
-
-    def plane(yd, cd):
-        return (zh * 8 + zlp * 2 + cd, yd, zhp)
-
-    zz = lax.rem(z + 14, 16)
-    sq = zz // 4
-    src_lay = (sq // 2) * 8 + lax.rem(zz, 4) * 2 + lax.rem(sq, 2)
-
-    def source(lower, yd):
-        return (src_lay + 16 * lower, yd, x)
-
-    def near(xd, yd):
-        return (lax.rem(xd, 4) * 8 + zl * 2 + c, lax.rem(yd, 4), zh)
+    xp = lax.rem(zh + 4 - lookup(SHIFT, pair), 4)
+
+    def plane(cd):
+        return (xp * 8 + zlp * 2 + cd, y, zhp)
+
+    task = lookup([PLANE.index(k) for k in range(16)], z)
+    shift = lookup(SHIFT, task)
+    j = lax.rem(x + shift, 4)
+
+    def source(lower):
+        return (task + 16 * lower, y, j)
+
+    def near(jd, yd):
+        return (lax.rem(jd + 4 - shift, 4) * 8 + zl * 2 + c, lax.rem(yd, 4), zh)
 
     cross = (lay + 1 - 2 * c, y, zh)
     partner = (lax.rem(lay + 16, 32), y, zh)
@@ -81,30 +94,22 @@
     def signal(device):
         pl.semaphore_signal(barrier, inc=1, device_id=device, device_id_type=MESH)
 
-    for yd in range(4):
-        signal(source(0, yd))
-    signal(source(1, y))
-    for cd in range(2):
-        signal(plane(y, cd))
-    signal(near(x + 1, y))
-    signal(near(x + 3, y))
-    signal(near(x, y + 1))
-    signal(near(x, y + 3))
+    for device in (source(0), source(1), plane(0), plane(1), partner):
+        signal(device)
+    for step in (1, 3):
+        signal(near(j + step, y))
+    for step in (1, 2, 3):
+        signal(near(j, y + step))
     signal(cross)
-    signal(partner)
+    load = pltpu.make_async_copy(tf_ref, fv, lsem)
+    load.start()
 
     rows8 = lax.broadcasted_iota(jnp.int32, gain_ref.shape, 0)
     own = jnp.sum(jnp.where(rows8 == mid_ref[0], gain_ref[...], 0.0), axis=0, keepdims=True)
     own_gain[...] = jnp.broadcast_to(own, own_gain.shape)
-    fts[...] = tf_ref[...].T
-
-    @pl.when(upper)
-    def _():
-        pl.semaphore_wait(barrier, 16)
-
-    @pl.when(jnp.logical_not(upper))
-    def _():
-        pl.semaphore_wait(barrier, 10)
+    load.wait()
+    fts[...] = fv[...].T
+    pl.semaphore_wait(barrier, 11)
 
     sends = []
     count = [0]
@@ -127,30 +132,29 @@
         return pl.ds(pl.multiple_of(index, size), size)
 
     mine = al(zh * blk, blk)
-    ycols = al(y * blk, blk)
+    halves = [pl.ds(0, half), pl.ds(half, half)]
 
     def upper_moves():
-        moves = []
-        for cd in range(2):
-            moves.append((rb_ref.at[pl.ds(cd * half, half), :], rb.at[:, mine], Z_RB, plane(y, cd)))
-        for cd in range(2):
-            moves.append((own_gain, wa, Z_WA, plane(y, cd)))
-        for yd in range(4):
-            for cd in range(2):
-                moves.append((fts.at[pl.ds((2 * yd + cd) * fine, fine), :], ft.at[:, ycols], Z_FT + y, plane(yd, cd)))
-        for cd in range(2):
-            moves.append((tb_ref.at[pl.ds(cd * half, half), :], tb.at[:, mine], Z_TB, plane(y, cd)))
+        moves = [(tb_ref.at[halves[1], :], tr, Z_TR, partner)]
+        for cd in range(2):
+            moves.append((rb_ref.at[halves[cd], :], rb.at[:, mine], Z_RB, plane(cd)))
+        for cd in range(2):
+            moves.append((own_gain, wa, Z_WA, plane(cd)))
+        for cd in range(2):
+            moves.append((fts.at[halves[cd], :], fr, Z_FT, plane(cd)))
+        moves.append((tb_ref.at[halves[0], :], tb.at[:, mine], Z_TB, plane(0)))
         moves.append((rf_ref, ra_ref, O_RA, partner))
         return moves
 
     def lower_moves():
         moves = []
         for cd in range(2):
-            moves.append((rf_ref.at[pl.ds(cd * half, half), :], rf.at[al((2 * y + cd) * half, half), :], Z_RF, plane(y, cd)))
-        for cd in range(2):
-            moves.append((own_gain, wb, Z_WB, plane(y, cd)))
-        for cd in range(2):
-            moves.append((tf_ref.at[pl.ds(cd * half, half), :], tf.at[:, mine], Z_TF, plane(y, cd)))
+            moves.append((rf_ref.at[halves[cd], :], rf.at[al((2 * y + cd) * half, half), :], Z_RF, plane(cd)))
+        for cd in range(2):
+            moves.append((own_gain, wb, Z_WB, plane(cd)))
+        moves.append((tr, tb.at[:, mine], Z_TB, plane(1)))
+        for cd in range(2):
+            moves.append((tf_ref.at[halves[cd], :], tf.at[:, mine], Z_TF, plane(cd)))
         return moves
 
     @pl.when(upper)
@@ -161,6 +165,8 @@
     @pl.when(jnp.logical_not(upper))
     def _():
         for slot, (src, dst, recv, device) in enumerate(lower_moves()):
+            if recv == Z_TB:
+                arrived(tr, Z_TR)
             copy_of(src, dst, slot, recv, device).start()
 
     count[0] = len(upper_moves())
@@ -195,7 +201,7 @@
         return near(a, y)
 
     def on_y(a):
-        return near(x, a)
+        return near(j, a)
 
     def col_part(buf):
         def part(p, h):
@@ -203,9 +209,9 @@
             return buf.at[rows, al(p * blk, blk)]
         return part
 
-    def row_part(buf, size, core):
+    def row_part(buf, size, base):
         def part(p, h):
-            start = (2 * p + core) * size
+            start = base(p)
             if h is None:
                 return buf.at[al(start, size), :]
             return buf.at[al(start + h * (size // 2), size // 2), :]
@@ -218,8 +224,8 @@
         for k, step in enumerate(ORDER):
             arrived(part(lax.rem(y + step, 4), None), base + k)
 
-    def y_gather(buf, size, base, cbase):
-        part = row_part(buf, size, c)
+    def y_gather(buf, size, place, base, cbase):
+        part = row_part(buf, size, lambda p: place(p, c))
         ring = Ring(part, y, on_y, base)
         ring.start()
         cross_send(part(y, None), cbase)
@@ -231,18 +237,24 @@
         yield
         ring.far()
         cross_send(part(ring.pos(2), None), cbase + 3)
-        cross_wait(row_part(buf, size, 1 - c), cbase)
+        cross_wait(row_part(buf, size, lambda p: place(p, 1 - c)), cbase)
         yield
 
-    rb_ring = Ring(col_part(rb), x, on_x, R_RB)
-    tb_ring = Ring(col_part(tb), x, on_x, R_TB)
-    tf_ring = Ring(col_part(tf), x, on_x, R_TF)
-    ss_ring = Ring(col_part(ss), x, on_x, R_SS)
-
-    arrived(rb.at[:, al(x * blk, blk)], Z_RB)
+    rb_ring = Ring(col_part(rb), j, on_x, R_RB)
+    tb_ring = Ring(col_part(tb), j, on_x, R_TB)
+    tf_ring = Ring(col_part(tf), j, on_x, R_TF)
+    ss_ring = Ring(col_part(ss), j, on_x, R_SS)
+
+    arrived(rb.at[:, al(j * blk, blk)], Z_RB)
     rb_ring.start()
     arrived(rf.at[al((2 * y + c) * half, half), :], Z_RF)
-    gather = y_gather(rf, half, R_RF, C_RF)
+    def rf_place(p, core):
+        return (2 * p + core) * half
+
+    def mt_place(p, core):
+        return (4 * core + p) * fine
+
+    gather = y_gather(rf, half, rf_place, R_RF, C_RF)
     next(gather)
     rb_ring.left()
     rb_ring.right()
@@ -255,7 +267,7 @@
     def mix(a, b, core):
         return a + core * (b - a), b + core * (a - b)
 
-    me_a, me_b = mix(x, y, c)
+    me_a, me_b = mix(j, y, c)
 
     def ppart(a, b, h, core):
         jj, ii = mix(a, b, core)
@@ -268,7 +280,7 @@
     def device_ab(a, b):
         return near(*mix(a, b, c))
 
-    pp[al((2 * y + c) * half, half), al(x * blk, blk)] = power
+    pp[al((2 * y + c) * half, half), al(j * blk, blk)] = power
     ring_a = Ring(lambda p, h: ppart(p, me_b, h, c), me_a, lambda a: device_ab(a, me_b), R_PA)
     rings_b = []
     for k, step in enumerate(ORDER):
@@ -296,36 +308,36 @@
     start_b(1)
     ring_a.right()
     start_b(2)
+    sides_b(0)
     ring_a.far()
     start_b(3)
-    sides_b(0)
     sides_b(1)
-    arrived(tb.at[:, al(x * blk, blk)], Z_TB)
-    tb_ring.start()
     sides_b(2)
     far_b(0)
+    arrived(fr, Z_FT)
+    ycols = al(y * blk, blk)
+    for step in (1, 2, 3):
+        to = lax.rem(y + step, 4)
+        send(fr.at[al(to * fine, fine), :], ft.at[:, ycols], R_FT + y, on_y(to))
+    ft[:, ycols] = fr[al(y * fine, fine), :]
+    sides_b(3)
     far_b(1)
-    sides_b(3)
-    arrived(tf.at[:, al(x * blk, blk)], Z_TF)
-    tf_ring.start()
-    tb_ring.left()
-    tb_ring.right()
     far_b(2)
     far_b(3)
-    tf_ring.left()
-    tf_ring.right()
-    tb_ring.far()
     arrived(wa, Z_WA)
     arrived(wb, Z_WB)
     weight = wa[...][0:1, :] * wb[...][0:1, :]
-    ss[:, al(x * blk, blk)] = dot3(split(tb[...] * weight), right, NN)
-    ss_ring.start()
-    oa, obb = mix(x, y, 1 - c)
+    for step in (1, 2, 3):
+        away = lax.rem(y + step, 4)
+        arrived(ft.at[:, al(away * blk, blk)], R_FT + away)
+    oa, obb = mix(j, y, 1 - c)
     for k, step in enumerate(ORDER):
         for m, other in enumerate(ORDER):
             arrived(ppart(lax.rem(oa + step, 4), lax.rem(obb + other, 4), None, 1 - c), C_PP + 4 * k + m)
-    for yd in range(4):
-        arrived(ft.at[:, pl.ds(yd * blk, blk)], Z_FT + yd)
+    arrived(tb.at[:, al(j * blk, blk)], Z_TB)
+    tb_ring.start()
+    arrived(tf.at[:, al(j * blk, blk)], Z_TF)
+    tf_ring.start()
     ph[...], plo[...] = split(pp[...])
     first = ft[...] * weight
 
@@ -333,23 +345,30 @@
         return first + dot3(split(value), (ph[...], plo[...]), NT)
 
     value = lax.fori_loop(0, 2, horner, first)
+    tb_ring.left()
+    tb_ring.right()
+    value = lax.fori_loop(0, NTERMS - 3, horner, value)
+    mt[al(mt_place(y, c), fine), :] = value
+    gather = y_gather(mt, fine, mt_place, R_MT, C_MT)
+    next(gather)
+    tb_ring.far()
+    ss[:, al(j * blk, blk)] = dot3(split(tb[...] * weight), right, NN)
+    ss_ring.start()
+    tf_ring.left()
+    tf_ring.right()
+    next(gather)
     ss_ring.left()
     ss_ring.right()
     tf_ring.far()
-    value = lax.fori_loop(0, NTERMS - 3, horner, value)
-    mt[al((2 * y + c) * fine, fine), :] = value
-    gather = y_gather(mt, fine, R_MT, C_MT)
-    next(gather)
-    ss_ring.far()
-    next(gather)
     next(gather)
 
     middle = split(mt[...])
     ot[...] = dot3(split(tf[...]), middle, NT)
     place = al(c * half, half)
-    send(ot, prim_ref.at[place, :], O_PRIM + c, source(1, y))
+    send(ot, prim_ref.at[place, :], O_PRIM + c, source(1))
+    ss_ring.far()
     ob[...] = dot3(split(ss[...]), middle, NT)
-    send(ob, prim_ref.at[place, :], O_PRIM + c, source(0, y))
+    send(ob, prim_ref.at[place, :], O_PRIM + c, source(0))
 
     for h in range(2):
         piece = prim_ref.at[pl.ds(h * half, half), :]
@@ -379,15 +398,15 @@
     order = interface_gain.shape[1]
     half = blk // 2
     fine = order // 32
-    anywhere = pl.BlockSpec(memory_space=pl.ANY)
+    hbm = pl.BlockSpec(memory_space=pltpu.HBM)
     vmem = pl.BlockSpec(memory_space=pltpu.VMEM)
     shape = jax.ShapeDtypeStruct((blk, blk), F32)
     reflect_own = reflect_fwd[0]
     prim, sec, reflect_peer = pl.pallas_call(
         kernel,
         out_shape=(shape, shape, shape),
-        in_specs=[anywhere, vmem, anywhere, anywhere, pl.BlockSpec(memory_space=pltpu.SMEM), vmem],
-        out_specs=(anywhere, anywhere, anywhere),
+        in_specs=[hbm, hbm, hbm, hbm, pl.BlockSpec(memory_space=pltpu.SMEM), vmem],
+        out_specs=(hbm, hbm, hbm),
         scratch_shapes=[
             pltpu.VMEM((half, order), F32),
             pltpu.VMEM((half, order), F32),
@@ -405,8 +424,12 @@
             pltpu.VMEM((8, order), F32),
             pltpu.VMEM((8, order), F32),
             pltpu.VMEM((blk, blk), F32),
+            pltpu.VMEM((blk, blk), F32),
+            pltpu.VMEM((half, blk), F32),
+            pltpu.VMEM((half, blk), F32),
             pltpu.SemaphoreType.DMA((N_SEND,)),
             pltpu.SemaphoreType.DMA((N_RECV,)),
+            pltpu.SemaphoreType.DMA,
         ],
         compiler_params=pltpu.CompilerParams(
             collective_id=0, has_side_effects=True, vmem_limit_bytes=48 * 1024 * 1024),

time: 167 us -> 134 us (0.80)
  the two profiles are of different devices: /device:TPU:39 before, /device:TPU:46 now
where the time goes in v2:
time: 134 us; the launch traced here: 133 us
  Pallas kernels  127 us (95%)
  local copies, waits for them, and re-layouts  4.55 us (3%)
    pallas_call x1, Pallas kernels, on_device(): pl.pallas_call(kernel, out_shape=(shape, shape, shape), in_specs=[hbm, hb...  127 us
    unnamed x10, local copies, waits for them, and re-layouts  4.55 us

profile of v2, /device:TPU:46, one launch (start us, length us, event | category | flops | bytes accessed | tf_op | source)
XLA Modules:
  0.0 133.4 jit_solution(9827577181611105228)
XLA Ops:
  1.3 0.0 copy-start
  1.3 0.9 copy-done
  2.2 0.0 copy-start.1
  2.2 0.9 copy-done.1
  3.2 0.0 copy-start.2
  3.2 0.9 copy-done.2
  4.1 0.0 copy-start.3
  4.1 0.9 copy-done.3
  5.1 0.0 copy-start.4
  5.1 0.8 copy-done.4
  5.8 126.7 %star.1 = (f32[256,256]{1,0:T(8,128)S(1)}, f32[256,256]{1,0:T(8,128)S(1)}, f32[256,256]{1,0:T(8,128)S(1)}) custom-call(f32[256,256]{1,0:T(8,128)S(1)} %bitcast.9, f32[256,256]{1,0:T(8,128)S(1)} %bitcast.10, f32[256,256]{1,0:T(8,128)S(1)} %bitcast.11, f32[256,256]{1,0:T(8,128)S(1)} %bitcast.12, s32[1]{0:T(128)S(6)} %copy.8.mid_ref, f32[8,1024]{1,0:T(8,128)S(1)} %copy-done.4), custom_call_target="tpu_custom_call" | custom-call | tf_op jit(solution)/shard_map/star/pallas_call | solution.py:405
  132.5 0.9 select_bitcast_fusion
Async XLA Ops:
  1.3 1.0 copy-start
  2.2 0.9 copy-start.1
  3.2 0.9 copy-start.2
  4.1 0.9 copy-start.3
  5.1 0.8 copy-start.4

commit v3 on v2

--- a/solution.py
+++ b/solution.py
@@ -11,15 +11,14 @@
 BF16 = jnp.bfloat16
 ORDER = (0, 3, 1, 2)
 
-PLANE = (13, 10, 2, 4, 8, 1, 14, 6, 11, 3, 7, 12, 5, 15, 9, 0)
-SHIFT = (0, 3, 3, 0, 3, 3, 0, 2, 1, 2, 1, 2, 1, 2, 0, 0)
+PLANE = (3, 11, 2, 15, 5, 7, 9, 13, 14, 1, 0, 6, 8, 4, 12, 10)
+PLACE = (3, 1, 2, 3, 1, 2, 5, 0, 4, 7, 0, 3, 0, 0, 2, 7)
 
 Z_RB, Z_TB, Z_RF, Z_TF, Z_FT, Z_TR, Z_WA, Z_WB = 0, 1, 2, 3, 4, 5, 8, 9
 R_RB, R_TB, R_TF, R_SS, R_RF, R_MT, R_PA, R_PB = 10, 14, 18, 22, 26, 30, 34, 38
 C_RF, C_MT, C_PP = 54, 58, 62
-O_PRIM, O_SEC, O_RA = 78, 80, 82
-R_FT = 83
-N_RECV = 87
+O_MD, O_T, O_R, O_RA, R_FT = 78, 82, 86, 90, 91
+N_RECV = 95
 N_SEND = 120
 
 NN = (((1,), (0,)), ((), ()))
@@ -50,9 +49,9 @@
 
 
 def kernel(rf_ref, tf_ref, rb_ref, tb_ref, mid_ref, gain_ref,
-           prim_ref, sec_ref, ra_ref,
+           t_ref, r_ref, ra_ref,
            rb, tb, tf, ss, rf, pp, ph, plo, ft, mt, ot, ob, own_gain, wa, wb, fts,
-           fv, fr, tr, ssem, rsem, lsem):
+           fv, fr, tr, md, ssem, rsem, lsem):
     lay = lax.axis_index("layer")
     y = lax.axis_index("row")
     zh = lax.axis_index("col")
@@ -66,35 +65,45 @@
     wide = rf.shape[0]
     fine = ft.shape[0]
 
+    def spot(pair):
+        where = lookup(PLACE, pair)
+        turn = jnp.where(where < 4, 1, 3)
+        return turn, lax.rem(jnp.where(where < 4, 8 - where, where), 4)
+
+    def plane_of(pair):
+        zp = lookup(PLANE, pair)
+        turn, base = spot(pair)
+        xp = lax.rem(turn * zh + base, 4)
+        return [(xp * 8 + lax.rem(zp, 4) * 2 + cd, y, zp // 4) for cd in range(2)]
+
     upper = lay < 16
-    pair = lax.rem(lay, 16)
-    zp = lookup(PLANE, pair)
-    zhp = zp // 4
-    zlp = lax.rem(zp, 4)
-    xp = lax.rem(zh + 4 - lookup(SHIFT, pair), 4)
-
-    def plane(cd):
-        return (xp * 8 + zlp * 2 + cd, y, zhp)
+    plane = plane_of(lax.rem(lay, 16))
+
+    passes_t = jnp.logical_or(x == 1, x == 2)
+    passed = plane_of(jnp.where(passes_t, x - 1, lax.rem(x + 1, 4)) * 8 + lax.rem(lay, 8))
 
     task = lookup([PLANE.index(k) for k in range(16)], z)
-    shift = lookup(SHIFT, task)
-    j = lax.rem(x + shift, 4)
-
-    def source(lower):
-        return (task + 16 * lower, y, j)
+    turn, base = spot(task)
+    j = lax.rem(turn * (x + 4 - base), 4)
+
+    def source(dx):
+        return (lax.rem(task + 8 * dx, 32), y, j)
 
     def near(jd, yd):
-        return (lax.rem(jd + 4 - shift, 4) * 8 + zl * 2 + c, lax.rem(yd, 4), zh)
+        return (lax.rem(turn * jd + base, 4) * 8 + zl * 2 + c, lax.rem(yd, 4), zh)
+
+    def beside(dx):
+        return (lax.rem(lay + 8 * dx, 32), y, zh)
 
     cross = (lay + 1 - 2 * c, y, zh)
-    partner = (lax.rem(lay + 16, 32), y, zh)
+    partner = beside(2)
 
     barrier = pltpu.get_barrier_semaphore()
 
     def signal(device):
         pl.semaphore_signal(barrier, inc=1, device_id=device, device_id_type=MESH)
 
-    for device in (source(0), source(1), plane(0), plane(1), partner):
+    for device in (source(0), source(2), *passed, partner):
         signal(device)
     for step in (1, 3):
         signal(near(j + step, y))
@@ -135,40 +144,49 @@
     halves = [pl.ds(0, half), pl.ds(half, half)]
 
     def upper_moves():
-        moves = [(tb_ref.at[halves[1], :], tr, Z_TR, partner)]
-        for cd in range(2):
-            moves.append((rb_ref.at[halves[cd], :], rb.at[:, mine], Z_RB, plane(cd)))
-        for cd in range(2):
-            moves.append((own_gain, wa, Z_WA, plane(cd)))
-        for cd in range(2):
-            moves.append((fts.at[halves[cd], :], fr, Z_FT, plane(cd)))
-        moves.append((tb_ref.at[halves[0], :], tb.at[:, mine], Z_TB, plane(0)))
-        moves.append((rf_ref, ra_ref, O_RA, partner))
+        moves = []
+        for cd in range(2):
+            moves.append((rb_ref.at[halves[cd], :], rb.at[:, mine], Z_RB, plane[cd]))
+        moves.append((tb_ref.at[halves[1], :], tr, Z_TR, partner))
+        for cd in range(2):
+            moves.append((own_gain.at[pl.ds(0, 1), :], wa.at[pl.ds(0, 1), :], Z_WA, plane[cd]))
+        for cd in range(2):
+            moves.append((fts.at[halves[cd], :], fr, Z_FT, plane[cd]))
+        moves.append((tb_ref.at[halves[0], :], tb.at[:, mine], Z_TB, plane[0]))
         return moves
 
     def lower_moves():
         moves = []
         for cd in range(2):
-            moves.append((rf_ref.at[halves[cd], :], rf.at[al((2 * y + cd) * half, half), :], Z_RF, plane(cd)))
-        for cd in range(2):
-            moves.append((own_gain, wb, Z_WB, plane(cd)))
-        moves.append((tr, tb.at[:, mine], Z_TB, plane(1)))
-        for cd in range(2):
-            moves.append((tf_ref.at[halves[cd], :], tf.at[:, mine], Z_TF, plane(cd)))
+            moves.append((rf_ref.at[halves[cd], :], rf.at[al((2 * y + cd) * half, half), :], Z_RF, plane[cd]))
+        for cd in range(2):
+            moves.append((own_gain.at[pl.ds(0, 1), :], wb.at[pl.ds(0, 1), :], Z_WB, plane[cd]))
+        moves.append((tr, tb.at[:, mine], Z_TB, plane[1]))
+        for cd in range(2):
+            moves.append((tf_ref.at[halves[cd], :], tf.at[:, mine], Z_TF, plane[cd]))
         return moves
 
-    @pl.when(upper)
-    def _():
-        for slot, (src, dst, recv, device) in enumerate(upper_moves()):
-            copy_of(src, dst, slot, recv, device).start()
-
-    @pl.when(jnp.logical_not(upper))
-    def _():
-        for slot, (src, dst, recv, device) in enumerate(lower_moves()):
-            if recv == Z_TB:
-                arrived(tr, Z_TR)
-            copy_of(src, dst, slot, recv, device).start()
-
+    def start_moves(first, last):
+        @pl.when(upper)
+        def _():
+            for slot, (src, dst, recv, device) in list(enumerate(upper_moves()))[first:last]:
+                copy_of(src, dst, slot, recv, device).start()
+
+        @pl.when(jnp.logical_not(upper))
+        def _():
+            for slot, (src, dst, recv, device) in list(enumerate(lower_moves()))[first:last]:
+                if recv != Z_TB:
+                    copy_of(src, dst, slot, recv, device).start()
+
+    def relay_move():
+        @pl.when(jnp.logical_not(upper))
+        def _():
+            for slot, (src, dst, recv, device) in enumerate(lower_moves()):
+                if recv == Z_TB:
+                    arrived(tr, Z_TR)
+                    copy_of(src, dst, slot, recv, device).start()
+
+    start_moves(0, 2)
     count[0] = len(upper_moves())
 
     class Ring:
@@ -237,6 +255,7 @@
         yield
         ring.far()
         cross_send(part(ring.pos(2), None), cbase + 3)
+        yield
         cross_wait(row_part(buf, size, lambda p: place(p, 1 - c)), cbase)
         yield
 
@@ -261,36 +280,27 @@
     next(gather)
     rb_ring.far()
     next(gather)
+    next(gather)
     right = split(rf[...])
     power = dot3(split(rb[...]), right, NN)
 
-    def mix(a, b, core):
-        return a + core * (b - a), b + core * (a - b)
-
-    me_a, me_b = mix(j, y, c)
-
-    def ppart(a, b, h, core):
-        jj, ii = mix(a, b, core)
+    def ppart(jj, ii, h, core):
         start = (2 * ii + core) * half
-        cols = al(jj * blk, blk)
+        cols = al(lax.rem(jj, 4) * blk, blk)
         if h is None:
             return pp.at[al(start, half), cols]
         return pp.at[al(start + h * quarter, quarter), cols]
 
-    def device_ab(a, b):
-        return near(*mix(a, b, c))
-
     pp[al((2 * y + c) * half, half), al(j * blk, blk)] = power
-    ring_a = Ring(lambda p, h: ppart(p, me_b, h, c), me_a, lambda a: device_ab(a, me_b), R_PA)
-    rings_b = []
-    for k, step in enumerate(ORDER):
-        a = lax.rem(me_a + step, 4)
-        rings_b.append(Ring(
-            lambda p, h, a=a: ppart(a, p, h, c), me_b, lambda b: device_ab(me_a, b), R_PB + 4 * k))
+    ring_a = Ring(lambda p, h: ppart(p, y, h, c), j, on_x, R_PA)
+    rings_b = [
+        Ring(lambda p, h, jj=j + step: ppart(jj, p, h, c), y, on_y, R_PB + 4 * k)
+        for k, step in enumerate(ORDER)
+    ]
 
     def start_b(k):
         rings_b[k].start()
-        cross_send(rings_b[k].part(me_b, None), C_PP + 4 * k)
+        cross_send(rings_b[k].part(y, None), C_PP + 4 * k)
 
     def sides_b(k):
         rings_b[k].left()
@@ -307,47 +317,48 @@
     ring_a.left()
     start_b(1)
     ring_a.right()
+    start_moves(2, None)
     start_b(2)
     sides_b(0)
     ring_a.far()
     start_b(3)
+    relay_move()
     sides_b(1)
+    far_b(0)
     sides_b(2)
-    far_b(0)
+    far_b(1)
+    sides_b(3)
+    far_b(2)
+    far_b(3)
     arrived(fr, Z_FT)
     ycols = al(y * blk, blk)
     for step in (1, 2, 3):
         to = lax.rem(y + step, 4)
         send(fr.at[al(to * fine, fine), :], ft.at[:, ycols], R_FT + y, on_y(to))
     ft[:, ycols] = fr[al(y * fine, fine), :]
-    sides_b(3)
-    far_b(1)
-    far_b(2)
-    far_b(3)
-    arrived(wa, Z_WA)
-    arrived(wb, Z_WB)
-    weight = wa[...][0:1, :] * wb[...][0:1, :]
+    arrived(wa.at[pl.ds(0, 1), :], Z_WA)
+    arrived(wb.at[pl.ds(0, 1), :], Z_WB)
+    weight = wa[0:1, :] * wb[0:1, :]
+    for k, step in enumerate(ORDER):
+        for m, other in enumerate(ORDER):
+            arrived(ppart(j + step, lax.rem(y + other, 4), None, 1 - c), C_PP + 4 * k + m)
+    ph[...], plo[...] = split(pp[...])
+    arrived(tb.at[:, al(j * blk, blk)], Z_TB)
+    tb_ring.start()
     for step in (1, 2, 3):
         away = lax.rem(y + step, 4)
         arrived(ft.at[:, al(away * blk, blk)], R_FT + away)
-    oa, obb = mix(j, y, 1 - c)
-    for k, step in enumerate(ORDER):
-        for m, other in enumerate(ORDER):
-            arrived(ppart(lax.rem(oa + step, 4), lax.rem(obb + other, 4), None, 1 - c), C_PP + 4 * k + m)
-    arrived(tb.at[:, al(j * blk, blk)], Z_TB)
-    tb_ring.start()
+    first = ft[...] * weight
+
+    def horner(step, value):
+        return first + dot3(split(value), (ph[...], plo[...]), NT)
+
+    value = lax.fori_loop(0, NTERMS - 3, horner, first)
     arrived(tf.at[:, al(j * blk, blk)], Z_TF)
     tf_ring.start()
-    ph[...], plo[...] = split(pp[...])
-    first = ft[...] * weight
-
-    def horner(step, value):
-        return first + dot3(split(value), (ph[...], plo[...]), NT)
-
-    value = lax.fori_loop(0, 2, horner, first)
     tb_ring.left()
     tb_ring.right()
-    value = lax.fori_loop(0, NTERMS - 3, horner, value)
+    value = lax.fori_loop(0, 2, horner, value)
     mt[al(mt_place(y, c), fine), :] = value
     gather = y_gather(mt, fine, mt_place, R_MT, C_MT)
     next(gather)
@@ -359,23 +370,52 @@
     next(gather)
     ss_ring.left()
     ss_ring.right()
+    next(gather)
     tf_ring.far()
-    next(gather)
-
-    middle = split(mt[...])
-    ot[...] = dot3(split(tf[...]), middle, NT)
+
     place = al(c * half, half)
-    send(ot, prim_ref.at[place, :], O_PRIM + c, source(1))
+
+    def result(k, left, buf, dx):
+        h = lax.rem(c + k, 2)
+        middle = split(mt[al(h * half, half), :])
+        buf[k] = dot3(left, middle, NT)
+        send(buf.at[k], md.at[place, al(h * half, half)], O_MD + 2 * c + h, source(dx))
+
+    lower = split(tf[...])
+    result(0, lower, ot, 1)
+    next(gather)
+    result(1, lower, ot, 1)
     ss_ring.far()
-    ob[...] = dot3(split(ss[...]), middle, NT)
-    send(ob, prim_ref.at[place, :], O_PRIM + c, source(0))
-
-    for h in range(2):
-        piece = prim_ref.at[pl.ds(h * half, half), :]
-        arrived(piece, O_PRIM + h)
-        send(piece, sec_ref.at[pl.ds(h * half, half), :], O_SEC + h, partner)
-    for h in range(2):
-        arrived(sec_ref.at[pl.ds(h * half, half), :], O_SEC + h)
+    side = split(ss[...])
+    result(0, side, ob, 3)
+    result(1, side, ob, 3)
+
+    @pl.when(upper)
+    def _():
+        copy_of(rf_ref, ra_ref, N_SEND - 1, O_RA, partner).start()
+
+    def quarter_of(buf, core, h):
+        return buf.at[pl.ds(core * half, half), pl.ds(h * half, half)]
+
+    quarters = ((0, 0), (1, 1), (0, 1), (1, 0))
+    for n, (core, h) in enumerate(quarters):
+        arrived(quarter_of(md, core, h), O_MD + 2 * core + h)
+        for role, buf, recv in ((passes_t, t_ref, O_T), (jnp.logical_not(passes_t), r_ref, O_R)):
+            @pl.when(role)
+            def _(buf=buf, recv=recv, n=n, core=core, h=h):
+                for m, dx in enumerate((1, 3)):
+                    copy_of(quarter_of(md, core, h), quarter_of(buf, core, h), N_SEND - 9 + 2 * n + m,
+                            recv + 2 * core + h, beside(dx)).start()
+    for core, h in quarters:
+        arrived(quarter_of(t_ref, core, h), O_T + 2 * core + h)
+        arrived(quarter_of(r_ref, core, h), O_R + 2 * core + h)
+    for n, (core, h) in enumerate(quarters):
+        for m in range(2):
+            copy_of(quarter_of(md, core, h), quarter_of(md, core, h), N_SEND - 9 + 2 * n + m, 0, cross).wait_send()
+
+    @pl.when(upper)
+    def _():
+        copy_of(rf_ref, ra_ref, N_SEND - 1, O_RA, partner).wait_send()
 
     @pl.when(upper)
     def _():
@@ -390,7 +430,7 @@
 
     for copy in sends:
         copy.wait_send()
-    assert count[0] <= N_SEND
+    assert count[0] <= N_SEND - 9
 
 
 def on_device(reflect_fwd, transmit_fwd, reflect_bwd, transmit_bwd, material_ids, interface_gain):
@@ -402,7 +442,7 @@
     vmem = pl.BlockSpec(memory_space=pltpu.VMEM)
     shape = jax.ShapeDtypeStruct((blk, blk), F32)
     reflect_own = reflect_fwd[0]
-    prim, sec, reflect_peer = pl.pallas_call(
+    trans, bounce, reflect_peer = pl.pallas_call(
         kernel,
         out_shape=(shape, shape, shape),
         in_specs=[hbm, hbm, hbm, hbm, pl.BlockSpec(memory_space=pltpu.SMEM), vmem],
@@ -418,8 +458,8 @@
             pltpu.VMEM((order, order), BF16),
             pltpu.VMEM((fine, order), F32),
             pltpu.VMEM((blk, order), F32),
-            pltpu.VMEM((half, blk), F32),
-            pltpu.VMEM((half, blk), F32),
+            pltpu.VMEM((2, half, half), F32),
+            pltpu.VMEM((2, half, half), F32),
             pltpu.VMEM((8, order), F32),
             pltpu.VMEM((8, order), F32),
             pltpu.VMEM((8, order), F32),
@@ -427,6 +467,7 @@
             pltpu.VMEM((blk, blk), F32),
             pltpu.VMEM((half, blk), F32),
             pltpu.VMEM((half, blk), F32),
+            pltpu.VMEM((blk, blk), F32),
             pltpu.SemaphoreType.DMA((N_SEND,)),
             pltpu.SemaphoreType.DMA((N_RECV,)),
             pltpu.SemaphoreType.DMA,
@@ -437,9 +478,7 @@
     )(reflect_own, transmit_fwd[0], reflect_bwd[0], transmit_bwd[0], material_ids, interface_gain)
     upper = lax.axis_index("layer") < lax.axis_size("layer") // 2
     reflect_a = jnp.where(upper, reflect_own, reflect_peer)
-    refl_out = reflect_a + jnp.where(upper, prim, sec)
-    trans_out = jnp.where(upper, sec, prim)
-    return (refl_out[None], trans_out[None])
+    return ((reflect_a + bounce)[None], trans[None])
 
 
 def solution(mesh):

time: 134 us -> 125 us (0.933)
  the two profiles are of different devices: /device:TPU:46 before, /device:TPU:99 now
where the time goes in v3:
time: 125 us; the launch traced here: 124 us
  Pallas kernels  117 us (94%)
  local copies, waits for them, and re-layouts  5.25 us (4%)
  between operations  1.3 us (1%)
    pallas_call x1, Pallas kernels, on_device(): pl.pallas_call(kernel, out_shape=(shape, shape, shape), in_specs=[hbm, hb...  117 us
    unnamed x11, local copies, waits for them, and re-layouts  5.25 us

profile of v3, /device:TPU:99, one launch (start us, length us, event | category | flops | bytes accessed | tf_op | source)
XLA Modules:
  0.0 124.3 jit_solution(15392408164232838775)
XLA Ops:
  1.3 0.0 copy-start
  1.3 0.9 copy-done
  2.2 0.0 copy-start.1
  2.2 0.9 copy-done.1
  3.2 0.0 copy-start.2
  3.2 0.9 copy-done.2
  4.1 0.0 copy-start.3
  4.1 0.9 copy-done.3
  5.1 0.0 copy-start.4
  5.1 0.8 copy-done.4
  5.8 117.0 %star.1 = (f32[256,256]{1,0:T(8,128)S(1)}, f32[256,256]{1,0:T(8,128)S(1)}, f32[256,256]{1,0:T(8,128)S(1)}) custom-call(f32[256,256]{1,0:T(8,128)S(1)} %bitcast.8, f32[256,256]{1,0:T(8,128)S(1)} %bitcast.10, f32[256,256]{1,0:T(8,128)S(1)} %bitcast.11, f32[256,256]{1,0:T(8,128)S(1)} %bitcast.12, s32[1]{0:T(128)S(6)} %copy.9.mid_ref, f32[8,1024]{1,0:T(8,128)S(1)} %copy-done.4), custom_call_target="tpu_custom_call" | custom-call | tf_op jit(solution)/shard_map/star/pallas_call | solution.py:445
  122.8 0.8 add_bitcast_fusion
  123.6 0.7 copy.10
Async XLA Ops:
  1.3 1.0 copy-start
  2.2 0.9 copy-start.1
  3.2 0.9 copy-start.2
  4.1 0.9 copy-start.3
  5.1 0.8 copy-start.4

commit v4 on v3

--- a/solution.py
+++ b/solution.py
@@ -166,7 +166,10 @@
             moves.append((tf_ref.at[halves[cd], :], tf.at[:, mine], Z_TF, plane[cd]))
         return moves
 
-    def start_moves(first, last):
+    def start_moves(first, last, lf=None, ll=None):
+        lf = first if lf is None else lf
+        ll = last if ll is None else ll
+
         @pl.when(upper)
         def _():
             for slot, (src, dst, recv, device) in list(enumerate(upper_moves()))[first:last]:
@@ -174,7 +177,7 @@
 
         @pl.when(jnp.logical_not(upper))
         def _():
-            for slot, (src, dst, recv, device) in list(enumerate(lower_moves()))[first:last]:
+            for slot, (src, dst, recv, device) in list(enumerate(lower_moves()))[lf:ll]:
                 if recv != Z_TB:
                     copy_of(src, dst, slot, recv, device).start()
 
@@ -275,6 +278,7 @@
 
     gather = y_gather(rf, half, rf_place, R_RF, C_RF)
     next(gather)
+    start_moves(2, 3)
     rb_ring.left()
     rb_ring.right()
     next(gather)
@@ -317,12 +321,12 @@
     ring_a.left()
     start_b(1)
     ring_a.right()
-    start_moves(2, None)
+    relay_move()
+    start_moves(3, None)
     start_b(2)
     sides_b(0)
     ring_a.far()
     start_b(3)
-    relay_move()
     sides_b(1)
     far_b(0)
     sides_b(2)
@@ -478,7 +482,8 @@
     )(reflect_own, transmit_fwd[0], reflect_bwd[0], transmit_bwd[0], material_ids, interface_gain)
     upper = lax.axis_index("layer") < lax.axis_size("layer") // 2
     reflect_a = jnp.where(upper, reflect_own, reflect_peer)
-    return ((reflect_a + bounce)[None], trans[None])
+    known = material_ids[0] >= 0
+    return ((reflect_a + bounce)[None], jnp.where(known, trans, bounce)[None])
 
 
 def solution(mesh):

time: 125 us -> 122 us (0.976)
  the two profiles are of different devices: /device:TPU:99 before, /device:TPU:1 now
where the time goes in v4:
time: 122 us
  Pallas kernels  115 us (94%)
  local copies, waits for them, and re-layouts  4.55 us (4%)
  between operations  1.31 us (1%)
    pallas_call x1, Pallas kernels, on_device(): pl.pallas_call(kernel, out_shape=(shape, shape, shape), in_specs=[hbm, hb...  115 us
    unnamed x10, local copies, waits for them, and re-layouts  4.55 us

profile of v4, /device:TPU:1, one launch (start us, length us, event | category | flops | bytes accessed | tf_op | source)
XLA Modules:
  0.0 121.6 jit_solution(18076014170645060106)
XLA Ops:
  1.3 0.0 copy-start
  1.3 0.9 copy-done
  2.2 0.0 copy-start.1
  2.2 0.9 copy-done.1
  3.2 0.0 copy-start.2
  3.2 0.9 copy-done.2
  4.1 0.0 copy-start.3
  4.1 0.9 copy-done.3
  5.1 0.0 copy-start.4
  5.1 0.8 copy-done.4
  5.8 114.9 %star.1 = (f32[256,256]{1,0:T(8,128)S(1)}, f32[256,256]{1,0:T(8,128)S(1)}, f32[256,256]{1,0:T(8,128)S(1)}) custom-call(f32[256,256]{1,0:T(8,128)S(1)} %bitcast.10, f32[256,256]{1,0:T(8,128)S(1)} %bitcast.11, f32[256,256]{1,0:T(8,128)S(1)} %bitcast.12, f32[256,256]{1,0:T(8,128)S(1)} %bitcast.13, s32[1]{0:T(128)S(6)} %copy.8.mid_ref, f32[8,1024]{1,0:T(8,128)S(1)} %copy-done.4), custom_call_target="tpu_custom_call" | custom-call | tf_op jit(solution)/shard_map/star/pallas_call | solution.py:449
  120.8 0.9 select_bitcast_fusion
Async XLA Ops:
  1.3 1.0 copy-start
  2.2 0.9 copy-start.1
  3.2 0.9 copy-start.2
  4.1 0.9 copy-start.3
  5.1 0.8 copy-start.4
